TPU v7x, 32 devices: a whole 2x2x4 slice. The times are simulated.
32 devices in a mesh: section: 2 (over y), expert: 16 (over z, x, core).
Axes of the slice: x: 2, y: 2, z: 4, core: 2. Of those that a mesh axis runs over, the one named last changes fastest.
Arguments:
- tokens: bfloat16 [2048, 7168], P('expert', 'section'), may hold values from -6 to 6
- exponents: int32 [2048, 56], P('expert', 'section'), may hold values from -9 to -5
- expert_ids: int32 [2048, 8], P('expert'), may hold values from 0 to 15, all different within a row; in each aligned block of 128 rows (0 to 127, 128 to 255, ...) at most 80 rows name the same one
- affinity: float32 [2048, 8], P('expert'), may hold values from 0.1 to 1
- w_gate: bfloat16 [16, 7168, 2048], P('expert', None, 'section'), may hold values from -0.0625 to 0.0625
- w_up: bfloat16 [16, 7168, 2048], P('expert', None, 'section'), may hold values from -0.0625 to 0.0625
- w_down: bfloat16 [16, 2048, 7168], P('expert', 'section'), may hold values from -0.125 to 0.125
Outputs:
- moe_out: bfloat16 [2048, 7168], P('expert', 'section')
Inputs may be any that keep to these rules, and one draw needn't show every extreme that they name: `expert_ids`: each row names 8 different experts. In the 128 rows of one token group no expert is named more than 80 times, a bound that some block reaches.
All inputs are finite; a program needn't handle non-finite values.
Results may differ from a plain program's by a relative error of at most 0.012.
Values may be sent and summed in bfloat16 or wider, within the bound.
No kernel may reach another device: no remote copies, remote signals or barrier semaphores. Data moves between devices by JAX's collectives and lax.ppermute only.
A program may use at most 192 MiB of HBM per device.

v0:
```python
import jax
import jax.numpy as jnp
from jax import lax
from jax.sharding import PartitionSpec as P

quant_limit = 448.0
route_scaling = 2.5


def slot_positions(ids, capacity, experts):
    flat = ids.reshape(-1)
    marks = (flat[:, None] == jnp.arange(experts, dtype=jnp.int32)[None, :]).astype(jnp.int32)
    before = jnp.cumsum(marks, axis=0) - marks
    slot = jnp.sum(before * marks, axis=1)
    return (flat * capacity + slot).reshape(ids.shape)


def body(tokens, exponents, expert_ids, affinity, w_gate, w_up, w_down):
    tok_rows, width = tokens.shape
    tile_count = width // 128
    top_count = expert_ids.shape[1]
    section_count = lax.axis_size("section")
    expert_count = lax.axis_size("expert")
    capacity = min(tok_rows, tok_rows * top_count * 5 // (4 * expert_count))
    slot_total = expert_count * capacity
    scales = jnp.exp2(exponents.astype(jnp.float32))
    tiles = tokens.astype(jnp.float32).reshape(tok_rows, tile_count, 128) / scales[:, :, None]
    quant = jnp.clip(tiles, -quant_limit, quant_limit).astype(jnp.bfloat16).reshape(tok_rows, width)
    slot_index = slot_positions(expert_ids, capacity, expert_count)
    columns = jnp.arange(slot_total, dtype=jnp.int32)
    select = jnp.any(slot_index[:, :, None] == columns[None, None, :], axis=1)
    contract = (((0,), (0,)), ((), ()))
    send_tiles = lax.dot_general(
        select.astype(jnp.bfloat16), quant, contract, preferred_element_type=jnp.float32
    ).astype(jnp.bfloat16)
    send_scales = lax.dot_general(
        select.astype(jnp.float32), scales, contract, precision=lax.Precision.HIGHEST
    ).astype(jnp.bfloat16)
    got_tiles, got_scales = (
        lax.all_to_all(
            send_tiles.reshape(expert_count, capacity, width),
            "expert",
            split_axis=0,
            concat_axis=0,
            tiled=True,
        ),
        lax.all_to_all(
            send_scales.reshape(expert_count, capacity, tile_count),
            "expert",
            split_axis=0,
            concat_axis=0,
            tiled=True,
        ),
    )
    all_tiles, all_scales = (
        lax.all_gather(got_tiles[None], "section", axis=0, tiled=True),
        lax.all_gather(got_scales[None], "section", axis=0, tiled=True),
    )
    restored = (
        all_tiles.reshape(section_count, expert_count, capacity, tile_count, 128)
        * all_scales[..., None]
    ).reshape(section_count, slot_total, width)
    hidden_local = w_gate.shape[2]
    gate = jnp.einsum(
        "srd,sdf->rf",
        restored,
        w_gate[0].reshape(section_count, width, hidden_local),
        preferred_element_type=jnp.float32,
    )
    up = jnp.einsum(
        "srd,sdf->rf",
        restored,
        w_up[0].reshape(section_count, width, hidden_local),
        preferred_element_type=jnp.float32,
    )
    hidden = (jax.nn.silu(gate) * up).astype(jnp.bfloat16)
    partial_rows = jnp.einsum(
        "rf,fsd->srd",
        hidden,
        w_down[0].reshape(hidden_local, section_count, width),
        preferred_element_type=jnp.float32,
    ).astype(jnp.bfloat16)
    summed = lax.psum_scatter(partial_rows, "section", scatter_dimension=0, tiled=True).astype(
        jnp.float32
    )
    summed_rows = summed.astype(jnp.bfloat16).reshape(expert_count, capacity, width)
    expert_rows = lax.all_to_all(summed_rows, "expert", split_axis=0, concat_axis=0, tiled=True)
    flat_rows = expert_rows.reshape(slot_total, width)
    picked = jnp.take(flat_rows, slot_index, axis=0)
    route_weight = route_scaling * affinity / jnp.sum(affinity, axis=1, keepdims=True)
    total = jnp.sum(picked.astype(jnp.float32) * route_weight[:, :, None], axis=1)
    return total.astype(jnp.bfloat16)


def solution(mesh):
    return jax.shard_map(
        body,
        mesh=mesh,
        in_specs=(
            P("expert", "section"),
            P("expert", "section"),
            P("expert", None),
            P("expert", None),
            P("expert", None, "section"),
            P("expert", None, "section"),
            P("expert", "section", None),
        ),
        out_specs=P("expert", "section"),
        check_vma=False,
    )
```

profile of v0, /device:TPU:11, one launch (start us, length us, event | category | flops | bytes accessed | tf_op | source)
XLA Modules:
  0.0 986.0 jit_solution(10012667298380749259)
XLA Ops:
  6.5 0.0 all-gather.4.cloned.1.call-start
  6.5 0.8 copy.61
  7.3 0.1 eq.42
  7.4 0.1 eq.38
  7.5 4.5 reduce-window.6
  12.0 0.1 slice.10
  12.1 0.1 copy.63
  12.3 0.1 copy.64
  12.4 0.1 broadcast_add_fusion
  12.5 0.1 reduce_sum.30
  12.6 1.3 compare_and_fusion
  13.9 0.1 copy.67
  14.0 0.5 copy-done
  14.5 1.6 fusion.6
  16.2 1.6 copy.68
  17.7 0.7 multiply_exponential_fusion
  18.4 0.2 fusion.9
  18.7 2.6 convolution_convert_fusion.1
  21.3 205.4 %all_to_all.15 = bf16[16,80,3584]{2,1,0:T(8,128)(2,1)} all-to-all(bf16[16,80,3584]{2,1,0:T(8,128)(2,1)S(1)} %bitcast.71), channel_id=1, replica_groups=mesh['section'=2,'expert'=16] {'expert'}, dimensions={0} | all-to-all | bytes 18350080 | tf_op jit(solution)/shard_map/all_to_all | solution.py:40
  226.7 0.0 all-gather.4.cloned.1.call-update
  226.7 0.7 copy-done.3
  227.4 0.3 convolution_convert_fusion.2
  227.7 0.2 reshape.59
  227.9 0.7 copy.69
  228.6 5.7 all-to-all-start.1
  234.2 0.0 reduce-scatter.2.cloned.1.call-start
  234.3 33.0 %reshape_squeeze.11 = bf16[1024,2,3584]{2,1,0:T(2,128)(2,1)} reshape(bf16[1,1024,7168]{2,1,0:T(8,128)(2,1)} %param.13) | data formatting | bytes 29360128 | tf_op jit(solution)/shard_map/reshape;squeeze | solution.py:80
  267.2 0.0 all-to-all-done.1
  267.3 8.5 all-gather.1
  275.8 0.4 copy.71
  276.2 13.6 %mul.47 = bf16[2,16,80,28,128]{4,3,2,1,0:T(8,128)(2,1)} broadcast(bf16[2,16,80,28]{3,2,1,0:T(8,128)(2,1)S(1)} %copy.71), dimensions={0,1,2,3} | broadcast | bytes 18493440 | tf_op jit(solution)/shard_map/mul | solution.py:60
  289.8 29.7 %mul.48 = bf16[2,1280,3584]{2,1,0:T(8,128)(2,1)} reshape(bf16[2,16,80,28,128]{4,3,2,1,0:T(8,128)(2,1)} %mul.47) | data formatting | bytes 36700160 | tf_op jit(solution)/shard_map/mul | solution.py:60
  319.5 128.6 %all-gather.4.cloned.1.call-done = bf16[32,80,3584]{2,1,0:T(8,128)(2,1)} async-done(((bf16[16,80,3584]{2,1,0:T(8,128)(2,1)}), bf16[32,80,3584]{2,1,0:T(8,128)(2,1)}) %all-gather.4.cloned.1.call-update) | async-done | bytes 18350096 | tf_op jit(solution)/shard_map/all_gather | solution.py:56
  448.1 12.9 %bitcast_multiply_fusion = bf16[2,1280,3584]{2,1,0:T(8,128)(2,1)S(1)} fusion(bf16[2,1280,3584]{2,1,0:T(8,128)(2,1)} %mul.48, bf16[2,1280,3584]{2,1,0:T(8,128)(2,1)} %bitcast.72), kind=kLoop, calls=%fused_computation.2 | loop fusion | flops 9175040 | bytes 55050240 | tf_op jit(solution)/shard_map/mul | solution.py:60
  461.0 23.7 %fusion.15 = f32[1280,1024,1]{1,0,2:T(8,128)} fusion(bf16[2,1280,3584]{2,1,0:T(8,128)(2,1)S(1)} %bitcast_multiply_fusion, bf16[2,3584,1024]{2,1,0:T(8,128)(2,1)} %bitcast.77), kind=kOutput, calls=%fused_computation.37 | convolution fusion | flops 18790481920 | bytes 38273024 | tf_op jit(solution)/shard_map/srd,sdf->rf/dot_general | solution.py:70
  484.7 23.6 %fusion.7 = bf16[1280,1024,1]{1,0,2:T(8,128)(2,1)S(1)} fusion(f32[1280,1024,1]{1,0,2:T(8,128)} %fusion.15, bf16[2,1280,3584]{2,1,0:T(8,128)(2,1)S(1)} %bitcast_multiply_fusion, bf16[2,3584,1024]{2,1,0:T(8,128)(2,1)} %bitcast.78), kind=kOutput, calls=%fused_computation.17 | convolution fusion | flops 18798346240 | bytes 40894464 | tf_op jit(solution)/shard_map/srd,sdf->rf/dot_general | solution.py:64
  508.2 26.9 %fusion = bf16[2,1280,3584]{2,1,0:T(8,128)(2,1)} fusion(bf16[1280,1024,1]{1,0,2:T(8,128)(2,1)S(1)} %fusion.7, bf16[1024,2,3584]{2,1,0:T(2,128)(2,1)} %reshape_squeeze.11), kind=kOutput, calls=%fused_computation.3 | convolution fusion | flops 18799656960 | bytes 35651584 | tf_op jit(solution)/shard_map/rf,fsd->srd/dot_general | solution.py:77
  535.1 0.0 reduce-scatter.2.cloned.1.call-update
  535.1 206.3 %reduce-scatter.2.cloned.1.call-done = bf16[1,1280,3584]{2,1,0:T(8,128)(2,1)} async-done(((bf16[2,1280,3584]{2,1,0:T(8,128)(2,1)}), bf16[1,1280,3584]{2,1,0:T(8,128)(2,1)}) %reduce-scatter.2.cloned.1.call-update) | async-done | bytes 9175056 | tf_op jit(solution)/shard_map/reduce_scatter | solution.py:83
  741.4 6.6 all-to-all-start.2
  748.0 0.1 copy.73
  748.1 0.1 reshape.64
  748.2 0.0 copy-done.4
  748.3 0.1 copy.66
  748.4 0.1 copy.74
  748.5 198.7 %all-to-all-done.2 = bf16[16,80,3584]{2,1,0:T(8,128)(2,1)} async-done(((bf16[16,80,3584]{2,1,0:T(8,128)(2,1)}), bf16[16,80,3584]{2,1,0:T(8,128)(2,1)}, u32[]{:S(2)}, u32[]{:S(2)}) %all-to-all-start.2) | async-done | bytes 9175072 | tf_op jit(solution)/shard_map/all_to_all | solution.py:87
  947.2 18.6 %gather_fusion = bf16[1024,3584]{1,0:T(8,128)(2,1)} fusion(bf16[1280,3584]{1,0:T(8,128)(2,1)} %bitcast.13, s32[1024]{0:T(1024)S(1)} %broadcast_clamp_fusion), kind=kCustom, calls=%fused_computation | custom fusion | bytes 14684160 | tf_op jit(solution)/shard_map/jit(_take)/gather | solution.py:89
  965.8 13.3 %multiply_reduce_fusion = bf16[128,3584]{1,0:T(8,128)(2,1)} fusion(bf16[1024,3584]{1,0:T(8,128)(2,1)} %gather_fusion, f32[128,8]{1,0:T(8,128)S(1)} %copy.74, pred[128,8]{1,0:T(8,128)(4,1)S(1)} %copy.66), kind=kLoop, calls=%fused_computation.6 | loop fusion | flops 14221312 | bytes 8262656 | tf_op jit(solution)/shard_map/reduce_sum | solution.py:91
  (17 shorter events, 0.2 us)
Async XLA Ops:
  6.5 441.5 %all-gather.4.cloned.1.call-start = ((), (), s32[]{:S(2)}) async-start(), calls=%async_computation.5 | async-start | bytes 27525120 | tf_op jit(solution)/shard_map/all_gather | solution.py:56
  13.9 0.6 copy-start
  226.7 0.7 copy-start.3
  228.6 38.7 %all-to-all-start.1 = ((bf16[16,80,28]{1,2,0:T(8,128)(2,1)}), bf16[16,80,28]{1,2,0:T(8,128)(2,1)S(1)}, u32[]{:S(2)}, u32[]{:S(2)}) async-start(bf16[16,80,28]{1,2,0:T(8,128)(2,1)} %copy.69), calls=%async_computation.1 | async-start | bytes 262144 | tf_op jit(solution)/shard_map/all_to_all | solution.py:47
  234.2 507.2 %reduce-scatter.2.cloned.1.call-start = ((), (), s32[]{:S(2)}) async-start(), calls=%async_computation.4 | async-start | bytes 27525120 | tf_op jit(solution)/shard_map/reduce_scatter | solution.py:83
  741.4 6.6 copy-start.1
  741.4 6.9 copy-start.4
  741.4 7.0 copy-start.2
  741.4 205.8 %all-to-all-start.2 = ((bf16[16,80,3584]{2,1,0:T(8,128)(2,1)}), bf16[16,80,3584]{2,1,0:T(8,128)(2,1)}, u32[]{:S(2)}, u32[]{:S(2)}) async-start(bf16[16,80,3584]{2,1,0:T(8,128)(2,1)} %bitcast.73), calls=%async_computation.3 | async-start | bytes 18350080 | tf_op jit(solution)/shard_map/all_to_all | solution.py:87
Sparse Core Ops, SparseCore 0:
  226.8 221.2 all-gather.3
  535.2 206.0 reduce-scatter.1
where the time goes:
time: 988 us; the launch traced here: 986 us
  waiting for transfers between devices  534 us (54%)
  blocking collectives  214 us (22%)
  local copies, waits for them, and re-layouts  101 us (10%)
  matrix products  77 us (8%)
  other arithmetic  34.8 us (4%)
  between operations  13.5 us (1%)
  starting transfers between devices  12.4 us (1%)
    reduce_scatter x1, waiting for transfers between devices, body(): lax.psum_scatter(partial_rows, 'section', scatter_dimension=0, tiled=True)  206 us
    all_to_all x1, blocking collectives, body(): lax.all_to_all(send_tiles.reshape(expert_count, capacity, width), 'expert...  205 us
    all_to_all x1, waiting for transfers between devices, body(): lax.all_to_all(summed_rows, 'expert', split_axis=0, concat_axis=0, tiled=...  199 us
    all_gather x1, waiting for transfers between devices, body(): lax.all_gather(got_tiles[None], 'section', axis=0, tiled=True)  129 us
    mul x2, local copies, waits for them, and re-layouts, body(): all_tiles.reshape(section_count, expert_count, capacity, tile_count, 128)  43.3 us
    another operation x1, local copies, waits for them, and re-layouts, body(): w_down[0].reshape(hidden_local, section_count, width)  33 us
    dot_general x1, matrix products, body(): jnp.einsum('rf,fsd->srd', hidden, w_down[0].reshape(hidden_local, section...  26.9 us
    dot_general x1, matrix products, body(): jnp.einsum('srd,sdf->rf', restored, w_up[0].reshape(section_count, width,...  23.7 us
  transfers between devices with their start and end apart: 4, of which 3 were waited for; matrix products, arithmetic and copies ran while one was open for 8% of the time, Pallas kernels for 0%

commit v1 on v0

--- a/solution.py
+++ b/solution.py
@@ -53,7 +53,12 @@
         ),
     )
     all_tiles, all_scales = (
-        lax.all_gather(got_tiles[None], "section", axis=0, tiled=True),
+        jnp.concatenate(
+            lax.all_to_all(
+                jnp.stack([got_tiles[None]] * lax.axis_size("section")), "section", 0, 0
+            ),
+            axis=0,
+        ),
         lax.all_gather(got_scales[None], "section", axis=0, tiled=True),
     )
     restored = (

time: 988 us -> 1050 us (1.063)
  waiting for transfers between devices: 534 us -> 603 us
  blocking collectives: 214 us -> 169 us
  starting transfers between devices: 12.4 us -> 28.4 us
  other arithmetic: 34.8 us -> 50.4 us
    all_to_all x1 -> x0, blocking collectives: 205 us -> none  [body(): lax.all_to_all(send_tiles.reshape(expert_count, capacity, width), 'expert...]
    all_to_all x0 -> x2, waiting for transfers between devices: none -> 198 us  [the longest x1 198 us: body(): lax.all_to_all(send_tiles.reshape(expert_count, capacity, width), 'expert...]
    all_gather x1, blocking collectives: 8.46 us -> 169 us  [body(): lax.all_gather(got_scales[None], 'section', axis=0, tiled=True)]
    all_gather x1 -> x0, waiting for transfers between devices: 129 us -> none  [body(): lax.all_gather(got_tiles[None], 'section', axis=0, tiled=True)]
    all_to_all x0 -> x2, starting transfers between devices: none -> 17 us  [the longest x1 10.3 us: body(): lax.all_to_all(jnp.stack([got_tiles[None]] * lax.axis_size('section')), '...]
    another operation x3 -> x4, other arithmetic: 4.64 us -> 20.3 us  [the longest x1 15.7 us: body(): jnp.stack([got_tiles[None]] * lax.axis_size('section'))]
  transfers between devices with their start and end apart: 4 -> 5, of which waited for: 3 -> 3; matrix products, arithmetic and copies ran while one was open for 8% -> 9% of each run, Pallas kernels for 0% -> 0%
where the time goes in v1:
time: 1050 us; the launch traced here: 1040 us
  waiting for transfers between devices  603 us (57%)
  blocking collectives  169 us (16%)
  local copies, waits for them, and re-layouts  99.4 us (9%)
  matrix products  80.6 us (8%)
  other arithmetic  50.4 us (5%)
  starting transfers between devices  28.4 us (3%)
  between operations  13.5 us (1%)
    reduce_scatter x1, waiting for transfers between devices, body(): lax.psum_scatter(partial_rows, 'section', scatter_dimension=0, tiled=True)  207 us
    all_to_all x1, waiting for transfers between devices, body(): lax.all_to_all(summed_rows, 'expert', split_axis=0, concat_axis=0, tiled=...  199 us
    all_to_all x1, waiting for transfers between devices, body(): lax.all_to_all(send_tiles.reshape(expert_count, capacity, width), 'expert...  198 us
    all_gather x1, blocking collectives, body(): lax.all_gather(got_scales[None], 'section', axis=0, tiled=True)  169 us
    mul x2, local copies, waits for them, and re-layouts, body(): all_tiles.reshape(section_count, expert_count, capacity, tile_count, 128)  43.5 us
    another operation x1, local copies, waits for them, and re-layouts, body(): w_down[0].reshape(hidden_local, section_count, width)  32 us
    dot_general x1, matrix products, body(): jnp.einsum('rf,fsd->srd', hidden, w_down[0].reshape(hidden_local, section...  26.9 us
    dot_general x1, matrix products, body(): jnp.einsum('srd,sdf->rf', restored, w_up[0].reshape(section_count, width,...  23.7 us
  transfers between devices with their start and end apart: 5, of which 3 were waited for; matrix products, arithmetic and copies ran while one was open for 9% of the time, Pallas kernels for 0%

profile of v1, /device:TPU:11, one launch (start us, length us, event | category | flops | bytes accessed | tf_op | source)
XLA Modules:
  0.0 1044.7 jit_solution(2486354130776963056)
XLA Ops:
  6.5 0.8 copy.61
  7.3 0.1 eq.42
  7.4 0.1 eq.38
  7.5 4.5 reduce-window.6
  12.0 0.1 slice.10
  12.1 0.1 copy.63
  12.3 0.1 copy.64
  12.4 0.1 broadcast_add_fusion
  12.5 0.1 reduce_sum.30
  12.6 1.2 compare_and_fusion
  13.8 0.1 copy.67
  13.9 0.5 copy-done
  14.4 1.6 fusion.6
  16.1 1.6 copy.68
  17.6 0.7 multiply_exponential_fusion
  18.4 0.2 fusion.9
  18.6 6.1 convolution_convert_fusion.1
  24.8 6.7 all-to-all-start
  31.4 0.3 convolution_convert_fusion.2
  31.7 0.2 reshape.55
  31.9 0.7 copy.69
  32.6 198.0 %all-to-all-done = bf16[16,80,3584]{2,1,0:T(8,128)(2,1)} async-done(((bf16[16,80,3584]{2,1,0:T(8,128)(2,1)}), bf16[16,80,3584]{2,1,0:T(8,128)(2,1)}, u32[]{:S(2)}, u32[]{:S(2)}) %all-to-all-start) | async-done | bytes 9175072 | tf_op jit(solution)/shard_map/all_to_all | solution.py:40
  230.6 4.8 all-to-all-start.2
  235.4 15.7 %pad_maximum_fusion = bf16[2,1,16,80,3584]{4,3,2,1,0:T(8,128)(2,1)} fusion(bf16[1,1,16,80,3584]{4,3,2,1,0:T(8,128)(2,1)} %bitcast.4), kind=kLoop, calls=%fused_computation.2 | loop fusion | flops 9175040 | bytes 27525120 | tf_op jit(solution)/shard_map/stack | solution.py:58
  251.1 0.0 all-to-all-done.2
  251.1 10.3 all-to-all-start.1
  261.4 0.0 reduce-scatter.2.cloned.1.call-start
  261.4 32.0 %reshape_squeeze.11 = bf16[1024,2,3584]{2,1,0:T(2,128)(2,1)} reshape(bf16[1,1024,7168]{2,1,0:T(8,128)(2,1)} %param.13) | data formatting | bytes 29360128 | tf_op jit(solution)/shard_map/reshape;squeeze | solution.py:85
  293.5 169.0 %all-gather = bf16[32,80,28]{1,0,2:T(8,128)(2,1)S(1)} all-gather(bf16[16,80,28]{1,0,2:T(8,128)(2,1)S(1)} %copy.70), channel_id=2, replica_groups=mesh['section'=2,'expert'=16] {'section'}, dimensions={0}, use_global_device_ids=true | all-gather | bytes 215040 | tf_op jit(solution)/shard_map/all_gather | solution.py:62
  462.5 0.4 copy.71
  463.0 13.8 %mul.47 = bf16[2,16,80,28,128]{4,3,2,1,0:T(8,128)(2,1)} broadcast(bf16[2,16,80,28]{3,2,1,0:T(8,128)(2,1)S(1)} %copy.71), dimensions={0,1,2,3} | broadcast | bytes 18493440 | tf_op jit(solution)/shard_map/mul | solution.py:65
  476.8 29.7 %mul.48 = bf16[2,1280,3584]{2,1,0:T(8,128)(2,1)} reshape(bf16[2,16,80,28,128]{4,3,2,1,0:T(8,128)(2,1)} %mul.47) | data formatting | bytes 36700160 | tf_op jit(solution)/shard_map/mul | solution.py:65
  506.4 0.0 all-to-all-done.1
  506.5 12.9 %bitcast_multiply_fusion = bf16[2,1280,3584]{2,1,0:T(8,128)(2,1)S(1)} fusion(bf16[2,1280,3584]{2,1,0:T(8,128)(2,1)} %mul.48, bf16[2,1,16,80,3584]{4,3,2,1,0:T(8,128)(2,1)} %all-to-all-done.1), kind=kLoop, calls=%fused_computation.3 | loop fusion | flops 9175040 | bytes 55050240 | tf_op jit(solution)/shard_map/mul | solution.py:65
  519.4 23.7 %fusion.15 = f32[1280,1024,1]{1,0,2:T(8,128)} fusion(bf16[2,1280,3584]{2,1,0:T(8,128)(2,1)S(1)} %bitcast_multiply_fusion, bf16[2,3584,1024]{2,1,0:T(8,128)(2,1)} %bitcast.76), kind=kOutput, calls=%fused_computation.38 | convolution fusion | flops 18790481920 | bytes 38273024 | tf_op jit(solution)/shard_map/srd,sdf->rf/dot_general | solution.py:75
  543.0 23.6 %fusion.7 = bf16[1280,1024,1]{1,0,2:T(8,128)(2,1)S(1)} fusion(f32[1280,1024,1]{1,0,2:T(8,128)} %fusion.15, bf16[2,1280,3584]{2,1,0:T(8,128)(2,1)S(1)} %bitcast_multiply_fusion, bf16[2,3584,1024]{2,1,0:T(8,128)(2,1)} %bitcast.77), kind=kOutput, calls=%fused_computation.18 | convolution fusion | flops 18798346240 | bytes 40894464 | tf_op jit(solution)/shard_map/srd,sdf->rf/dot_general | solution.py:69
  566.6 26.9 %fusion = bf16[2,1280,3584]{2,1,0:T(8,128)(2,1)} fusion(bf16[1280,1024,1]{1,0,2:T(8,128)(2,1)S(1)} %fusion.7, bf16[1024,2,3584]{2,1,0:T(2,128)(2,1)} %reshape_squeeze.11), kind=kOutput, calls=%fused_computation.4 | convolution fusion | flops 18799656960 | bytes 35651584 | tf_op jit(solution)/shard_map/rf,fsd->srd/dot_general | solution.py:82
  593.5 0.0 reduce-scatter.2.cloned.1.call-update
  593.5 206.6 %reduce-scatter.2.cloned.1.call-done = bf16[1,1280,3584]{2,1,0:T(8,128)(2,1)} async-done(((bf16[2,1280,3584]{2,1,0:T(8,128)(2,1)}), bf16[1,1280,3584]{2,1,0:T(8,128)(2,1)}) %reduce-scatter.2.cloned.1.call-update) | async-done | bytes 9175056 | tf_op jit(solution)/shard_map/reduce_scatter | solution.py:88
  800.1 6.6 all-to-all-start.3
  806.8 0.1 copy.73
  806.9 0.1 reshape.60
  807.0 0.1 copy.66
  807.1 0.0 copy-done.2
  807.2 0.1 copy.74
  807.3 198.7 %all-to-all-done.3 = bf16[16,80,3584]{2,1,0:T(8,128)(2,1)} async-done(((bf16[16,80,3584]{2,1,0:T(8,128)(2,1)}), bf16[16,80,3584]{2,1,0:T(8,128)(2,1)}, u32[]{:S(2)}, u32[]{:S(2)}) %all-to-all-start.3) | async-done | bytes 9175072 | tf_op jit(solution)/shard_map/all_to_all | solution.py:92
  1006.0 18.6 %gather_fusion = bf16[1024,3584]{1,0:T(8,128)(2,1)} fusion(bf16[1280,3584]{1,0:T(8,128)(2,1)} %bitcast.14, s32[1024]{0:T(1024)S(1)} %broadcast_clamp_fusion), kind=kCustom, calls=%fused_computation | custom fusion | bytes 14684160 | tf_op jit(solution)/shard_map/jit(_take)/gather | solution.py:94
  1024.6 13.3 %multiply_reduce_fusion = bf16[128,3584]{1,0:T(8,128)(2,1)} fusion(bf16[1024,3584]{1,0:T(8,128)(2,1)} %gather_fusion, f32[128,8]{1,0:T(8,128)S(1)} %copy.74, pred[128,8]{1,0:T(8,128)(4,1)S(1)} %copy.66), kind=kLoop, calls=%fused_computation.7 | loop fusion | flops 14221312 | bytes 8262656 | tf_op jit(solution)/shard_map/reduce_sum | solution.py:96
  (18 shorter events, 0.2 us)
Async XLA Ops:
  13.8 0.6 copy-start
  24.8 6.7 copy-start.3
  24.8 205.9 %all-to-all-start = ((bf16[16,80,3584]{2,1,0:T(8,128)(2,1)}), bf16[16,80,3584]{2,1,0:T(8,128)(2,1)}, u32[]{:S(2)}, u32[]{:S(2)}) async-start(bf16[16,80,3584]{2,1,0:T(8,128)(2,1)} %bitcast.71), calls=%async_computation | async-start | bytes 18350080 | tf_op jit(solution)/shard_map/all_to_all | solution.py:40
  230.6 20.5 %all-to-all-start.2 = ((bf16[16,80,28]{1,2,0:T(8,128)(2,1)}), bf16[16,80,28]{1,2,0:T(8,128)(2,1)S(1)}, u32[]{:S(2)}, u32[]{:S(2)}) async-start(bf16[16,80,28]{1,2,0:T(8,128)(2,1)} %copy.69), calls=%async_computation.2 | async-start | bytes 262144 | tf_op jit(solution)/shard_map/all_to_all | solution.py:47
  251.1 255.4 %all-to-all-start.1 = ((bf16[2,1,16,80,3584]{4,3,2,1,0:T(8,128)(2,1)}), bf16[2,1,16,80,3584]{4,3,2,1,0:T(8,128)(2,1)}, u32[]{:S(2)}, u32[]{:S(2)}) async-start(bf16[2,1,16,80,3584]{4,3,2,1,0:T(8,128)(2,1)} %pad_maximum_fusion), calls=%async_computation.1 | async-start | bytes 36700160 | tf_op jit(solution)/shard_map/all_to_all | solution.py:57
  261.4 538.7 %reduce-scatter.2.cloned.1.call-start = ((), (), s32[]{:S(2)}) async-start(), calls=%async_computation.5 | async-start | bytes 27525120 | tf_op jit(solution)/shard_map/reduce_scatter | solution.py:88
  800.1 6.6 copy-start.1
  800.1 6.9 copy-start.4
  800.1 7.0 copy-start.2
  800.1 205.8 %all-to-all-start.3 = ((bf16[16,80,3584]{2,1,0:T(8,128)(2,1)}), bf16[16,80,3584]{2,1,0:T(8,128)(2,1)}, u32[]{:S(2)}, u32[]{:S(2)}) async-start(bf16[16,80,3584]{2,1,0:T(8,128)(2,1)} %bitcast.72), calls=%async_computation.4 | async-start | bytes 18350080 | tf_op jit(solution)/shard_map/all_to_all | solution.py:92
Sparse Core Ops, SparseCore 0:
  593.6 206.4 reduce-scatter.1
